TPU v7x, 32 devices: a whole 2x2x4 slice. The times are simulated.
32 devices in a mesh: slab: 8 (over z, y), walk: 4 (over x, core).
Axes of the slice: x: 2, y: 2, z: 4, core: 2. Of those that a mesh axis runs over, the one named last changes fastest.
Arguments:
- bias_grid: float32 [32, 512, 512], P('slab', 'walk'), may hold values from 0 to 12, as said below
- hill_slab: int32 [64, 64, 1], P(('slab', 'walk')), may hold values from 0 to 7; in each aligned block of 128 rows (0 to 127, 128 to 255, ..., all dimensions but the last counted through in order) at most 64 rows name the same one
- hill_row: int32 [64, 64], P(('slab', 'walk')), may hold values from 0 to 3
- hill_col: int32 [64, 64], P(('slab', 'walk')), may hold values from 0 to 511
- hill_depth: int32 [64, 64], P(('slab', 'walk')), may hold values from 0 to 511
- hill_level: int32 [64, 64], P(('slab', 'walk')), may hold values from 0 to 7
- hill_count: int32 [64], P(('slab', 'walk')), may hold values from 1 to 64
- height_levels: float32 [8], replicated, may hold values from 0.5 to 2
Outputs:
- new_bias: float32 [32, 512, 512], P('slab', 'walk')
- free_energy: float32 [32, 512, 512], P('slab', 'walk')
Inputs may be any that keep to these rules, and one draw needn't show every extreme that they name: `bias_grid`: the bias is not negative. `hill_slab`: among the hills of one device's walkers (128 hills in a row of the flattened walkers and hills), no slab is named more than 64 times, and in some such blocks one slab is named exactly 64 times.
All inputs are finite; a program needn't handle non-finite values.
Results may differ from a plain program's by a relative error of at most 0.000082.
Values sent between devices are 32-bit elements; how exact they have to be, the bound alone decides.
A program may use at most 64 MiB of HBM per device.

v0:
```python
import math

import jax
import jax.numpy as jnp
from jax import lax
from jax.sharding import PartitionSpec as P

BASE_HEIGHT = 1.2
TEMPER = 4.0
SIGMA_SHARE = 0.3125
FREE_SCALE = 10.0 / 9.0


def from_behind(block, axis, distance):
    devices = range(lax.axis_size(axis))
    route = [((i - distance) % len(devices), i) for i in devices]
    return lax.ppermute(block, axis, route)


def gaussian(position, centre, extent, radius):
    offset = jnp.mod(position - centre + extent // 2, extent) - extent // 2
    inside = (offset >= -radius) & (offset < radius)
    spread = SIGMA_SHARE * radius
    distance = offset.astype(jnp.float32)
    return jnp.where(inside, jnp.exp(-(distance * distance) / (2.0 * spread * spread)), 0.0)


def deposit(row_ids, col_ids, depth_ids, hill_lists, grid_rows, grid_cols, grid_depth, radius):
    slot_total = hill_lists.shape[1]
    block_size = math.gcd(slot_total, 256)
    row_count = row_ids.shape[0]
    col_count = col_ids.shape[0]
    depth_count = depth_ids.shape[0]

    def one_block(carry_sum, index):
        portion = lax.dynamic_slice_in_dim(hill_lists, index * block_size, block_size, 1)
        row_gauss = (
            gaussian(row_ids[:, None], portion[1].astype(jnp.int32)[None, :], grid_rows, radius)
            * portion[0][None, :]
        )
        col_gauss = gaussian(
            col_ids[:, None], portion[2].astype(jnp.int32)[None, :], grid_cols, radius
        )
        depth_gauss = gaussian(
            depth_ids[None, :], portion[3].astype(jnp.int32)[:, None], grid_depth, radius
        )
        plane_gauss = (row_gauss[:, None, :] * col_gauss[None, :, :]).reshape(
            row_count * col_count, block_size
        )
        added = jnp.dot(
            plane_gauss,
            depth_gauss,
            precision=lax.Precision.HIGHEST,
            preferred_element_type=jnp.float32,
        )
        return (carry_sum + added, None)

    start = jnp.zeros((row_count * col_count, depth_count), jnp.float32)
    result, unused = lax.scan(one_block, start, jnp.arange(slot_total // block_size))
    return result.reshape(row_count, col_count, depth_count)


def per_device(
    bias_grid, hill_slab, hill_row, hill_col, hill_depth, hill_level, hill_count, height_levels
):
    rows_dev, cols_dev, depth_bins = bias_grid.shape
    slab_count = lax.axis_size("slab")
    walk_count = lax.axis_size("walk")
    radius = 2 * rows_dev
    grid_rows = rows_dev * slab_count
    grid_cols = cols_dev * walk_count
    walkers_dev, hill_slots = hill_row.shape
    sent_rows = walkers_dev * hill_slots
    capacity = max(2, 4 * sent_rows // slab_count)
    target = hill_slab[:, :, 0].reshape(-1)
    centre_row = target * rows_dev + hill_row.reshape(-1)
    is_live = (
        lax.broadcasted_iota(jnp.int32, (walkers_dev, hill_slots), 1) < hill_count[:, None]
    ).reshape(-1)
    level_match = hill_level.reshape(-1)[:, None] == lax.broadcasted_iota(
        jnp.int32, (1, height_levels.shape[0]), 1
    )
    base_height = jnp.sum(jnp.where(level_match, height_levels[None, :], 0.0), axis=1)
    base_height = jnp.where(is_live, BASE_HEIGHT * base_height, 0.0)
    same_slab = target[:, None] == target[None, :]
    earlier = lax.broadcasted_iota(jnp.int32, (sent_rows, sent_rows), 1) < lax.broadcasted_iota(
        jnp.int32, (sent_rows, sent_rows), 0
    )
    slot_rank = jnp.sum((same_slab & earlier).astype(jnp.int32), axis=1)
    slot_place = target * capacity + slot_rank
    placing = (
        slot_place[:, None] == lax.broadcasted_iota(jnp.int32, (1, slab_count * capacity), 1)
    ).astype(jnp.float32)
    fields = jnp.stack(
        [
            base_height,
            centre_row.astype(jnp.float32),
            hill_col.reshape(-1).astype(jnp.float32),
            hill_depth.reshape(-1).astype(jnp.float32),
        ]
    )
    outgoing = jnp.dot(
        fields, placing, precision=lax.Precision.HIGHEST, preferred_element_type=jnp.float32
    )
    outgoing = outgoing.reshape(4, slab_count, capacity)
    arrived = lax.all_to_all(outgoing, "slab", split_axis=1, concat_axis=1, tiled=True).reshape(
        4, slab_count * capacity
    )
    shared = lax.all_gather(arrived, "walk", axis=1, tiled=True)
    slab_index = lax.axis_index("slab")
    walk_index = lax.axis_index("walk")
    local_row = jnp.clip(shared[1].astype(jnp.int32) - slab_index * rows_dev, 0, rows_dev - 1)
    local_col = shared[2].astype(jnp.int32) - walk_index * cols_dev
    local_depth = jnp.clip(shared[3].astype(jnp.int32), 0, depth_bins - 1)
    owned = (local_col >= 0) & (local_col < cols_dev)
    flat_place = (
        local_row * cols_dev + jnp.clip(local_col, 0, cols_dev - 1)
    ) * depth_bins + local_depth
    picked = bias_grid.reshape(-1)[flat_place]
    centre_value = lax.psum(jnp.where(owned, picked, 0.0), "walk")
    height = shared[0] * jnp.exp(-centre_value / TEMPER)
    hill_lists = jnp.stack([height, shared[1], shared[2], shared[3]])
    col_ids = walk_index * cols_dev + lax.broadcasted_iota(jnp.int32, (cols_dev,), 0)
    depth_ids = lax.broadcasted_iota(jnp.int32, (depth_bins,), 0)
    collected = [hill_lists]
    for offset in (-2, -1, 1, 2):
        collected.append(from_behind(hill_lists, "slab", offset))
    row_ids = slab_index * rows_dev + lax.broadcasted_iota(jnp.int32, (rows_dev,), 0)
    added = deposit(
        row_ids,
        col_ids,
        depth_ids,
        jnp.concatenate(collected, axis=1),
        grid_rows,
        grid_cols,
        depth_bins,
        radius,
    )
    new_bias = bias_grid + added
    highest = lax.pmax(jnp.max(new_bias), ("slab", "walk"))
    free_energy = FREE_SCALE * (highest - new_bias)
    return (new_bias, free_energy)


def solution(mesh):
    in_specs = (
        P("slab", "walk", None),
        P(("slab", "walk"), None, None),
        P(("slab", "walk"), None),
        P(("slab", "walk"), None),
        P(("slab", "walk"), None),
        P(("slab", "walk"), None),
        P(("slab", "walk")),
        P(),
    )
    out_specs = (P("slab", "walk", None), P("slab", "walk", None))
    return jax.shard_map(
        per_device, mesh=mesh, in_specs=in_specs, out_specs=out_specs, check_vma=False
    )
```

profile of v0, /device:TPU:0, one launch (start us, length us, event | category | flops | bytes accessed | tf_op | source)
XLA Modules:
  0.0 229.3 jit_solution(4981247578799593196)
XLA Ops:
  7.1 7.3 %all-to-all-start = ((f32[8,1,256]{2,1,0:T(1,128)}), f32[8,1,256]{2,1,0:T(1,128)S(1)}, u32[]{:S(2)}, u32[]{:S(2)}) async-start(f32[8,1,256]{2,1,0:T(1,128)} %reshape.374), calls=%async_computation | async-start | bytes 16384 | tf_op jit(solution)/shard_map/all_to_all | solution.py:106
  15.9 5.0 %all-to-all-done = f32[8,1,256]{2,1,0:T(1,128)S(1)} async-done(((f32[8,1,256]{2,1,0:T(1,128)}), f32[8,1,256]{2,1,0:T(1,128)S(1)}, u32[]{:S(2)}, u32[]{:S(2)}) %all-to-all-start) | async-done | bytes 8224 | tf_op jit(solution)/shard_map/all_to_all | solution.py:106
  22.3 5.2 %all_gather.3 = f32[4,2048]{1,0:T(4,128)S(1)} all-gather(f32[4,512]{1,0:T(4,128)S(1)} %reshape.344), channel_id=1, replica_groups=mesh['slab'=8,'walk'=4] {'walk'}, dimensions={1}, use_global_device_ids=true | all-gather | bytes 40960 | tf_op jit(solution)/shard_map/all_gather | solution.py:109
  28.1 11.8 %gather_fusion = f32[2048]{0:T(1024)S(1)} fusion(f32[262144]{0:T(1024)S(1)} %bitcast.36, s32[2048]{0:T(1024)S(1)} %broadcast_clamp_fusion), kind=kCustom, calls=%fused_computation | custom fusion | bytes 24576 | tf_op jit(solution)/shard_map/gather | solution.py:119
  40.0 7.2 %psum.7 = f32[2048]{0:T(1024)S(1)} all-reduce(f32[2048]{0:T(1024)S(1)} %broadcast_select_fusion), channel_id=1, replica_groups=mesh['slab'=8,'walk'=4] {'walk'}, use_global_device_ids=true, to_apply=%region_2.3 | all-reduce | flops 2048 | bytes 16384 | tf_op jit(solution)/shard_map/psum | solution.py:120
  48.4 4.1 %collective-permute-start.1 = (f32[4,2048]{1,0:T(4,128)S(1)}, f32[4,2048]{1,0:T(4,128)S(1)}, u32[]{:S(2)}, u32[]{:S(2)}) collective-permute-start(f32[4,2048]{1,0:T(4,128)S(1)} %get-tuple-element.173), channel_id=1, source_target_pairs={{4,0},{8,4},{12,8},{16,12},{20,16},{24,20},{28,24},{0,28},{5,1},{9... | collective-permute-start | bytes 98312 | tf_op jit(solution)/shard_map/ppermute | solution.py:17
  54.5 3.8 %collective-permute-done.3 = f32[4,2048]{1,0:T(4,128)S(1)} collective-permute-done((f32[4,2048]{1,0:T(4,128)S(1)}, f32[4,2048]{1,0:T(4,128)S(1)}, u32[]{:S(2)}, u32[]{:S(2)}) %collective-permute-start.3) | collective-permute-done | bytes 32800 | tf_op jit(solution)/shard_map/ppermute | solution.py:17
  58.3 131.3 %while.14 = (s32[]{:T(128)}, f32[512,512]{1,0:T(8,128)S(1)}, s32[40]{0:T(128)S(1)}, f32[4,10240]{1,0:T(4,128)S(1)}, s32[]{:T(128)}, /*index=5*/s32[]{:T(128)}, s...) while((s32[]{:T(128)}, f32[512,512]{1,0:T(8,128)S(1)}, ...), condition=%wide.region_4.5_spmd.clone, body=%wide.region_3.4_spmd.clone.sunk | while | flops 809590656 | bytes 3429669 | solution.py:59
  73.0 1.7 convolution_add_fusion.2
  82.9 1.7 convolution_add_fusion.2
  86.1 1.7 convolution_add_fusion.2
  96.0 1.7 convolution_add_fusion.2
  99.3 1.7 convolution_add_fusion.2
  109.1 1.7 convolution_add_fusion.2
  112.4 1.7 convolution_add_fusion.2
  122.2 1.7 convolution_add_fusion.2
  125.5 1.7 convolution_add_fusion.2
  135.4 1.7 convolution_add_fusion.2
  138.7 1.7 convolution_add_fusion.2
  148.5 1.7 convolution_add_fusion.2
  151.8 1.7 convolution_add_fusion.2
  161.6 1.7 convolution_add_fusion.2
  190.5 37.0 %pmax.7 = f32[]{:T(128)} all-reduce(f32[]{:T(128)} %get-tuple-element.170), channel_id=1, replica_groups=mesh['slab'=8,'walk'=4] {'slab','walk'}, use_global_device_ids=true, to_apply=%region_6.7 | all-reduce | flops 1 | bytes 8 | tf_op jit(solution)/shard_map/pmax | solution.py:140
  227.5 1.8 subtract_multiply_fusion
  (373 shorter events, 96.6 us)
Async XLA Ops:
  0.6 0.8 copy-start.6
  1.4 0.7 copy-start.7
  2.1 0.7 copy-start.4
  2.8 0.7 copy-start.5
  3.6 0.7 copy-start.3
  5.3 0.7 copy-start.8
  7.1 13.8 %all-to-all-start = ((f32[8,1,256]{2,1,0:T(1,128)}), f32[8,1,256]{2,1,0:T(1,128)S(1)}, u32[]{:S(2)}, u32[]{:S(2)}) async-start(f32[8,1,256]{2,1,0:T(1,128)} %reshape.374), calls=%async_computation | async-start | bytes 16384 | tf_op jit(solution)/shard_map/all_to_all | solution.py:106
  27.4 0.6 copy-start.2
  39.9 7.2 %slice-start = ((f32[4,2048]{1,0:T(4,128)}), f32[1,2048]{1,0:T(1,128)S(1)}, s32[]{:S(2)}) async-start(f32[4,2048]{1,0:T(4,128)} %copy-done.2), calls=%async_computation.1 | async-start | bytes 16384 | tf_op jit(solution)/shard_map/slice | solution.py:121
  47.2 5.3 %collective-permute-start = (f32[4,2048]{1,0:T(4,128)S(1)}, f32[4,2048]{1,0:T(4,128)S(1)}, u32[]{:S(2)}, u32[]{:S(2)}) collective-permute-start(f32[4,2048]{1,0:T(4,128)S(1)} %get-tuple-element.173), channel_id=1, source_target_pairs={{8,0},{12,4},{16,8},{20,12},{24,16},{28,20},{0,24},{4,28},{9,1},{1... | collective-permute-start | bytes 98312 | tf_op jit(solution)/shard_map/ppermute | solution.py:17
  47.8 6.6 %collective-permute-start.2 = (f32[4,2048]{1,0:T(4,128)S(1)}, f32[4,2048]{1,0:T(4,128)S(1)}, u32[]{:S(2)}, u32[]{:S(2)}) collective-permute-start(f32[4,2048]{1,0:T(4,128)S(1)} %get-tuple-element.173), channel_id=1, source_target_pairs={{28,0},{0,4},{4,8},{8,12},{12,16},{16,20},{20,24},{24,28},{29,1},{... | collective-permute-start | bytes 98312 | tf_op jit(solution)/shard_map/ppermute | solution.py:17
  48.4 5.7 %collective-permute-start.1 = (f32[4,2048]{1,0:T(4,128)S(1)}, f32[4,2048]{1,0:T(4,128)S(1)}, u32[]{:S(2)}, u32[]{:S(2)}) collective-permute-start(f32[4,2048]{1,0:T(4,128)S(1)} %get-tuple-element.173), channel_id=1, source_target_pairs={{4,0},{8,4},{12,8},{16,12},{20,16},{24,20},{28,24},{0,28},{5,1},{9... | collective-permute-start | bytes 98312 | tf_op jit(solution)/shard_map/ppermute | solution.py:17
  52.6 5.7 %collective-permute-start.3 = (f32[4,2048]{1,0:T(4,128)S(1)}, f32[4,2048]{1,0:T(4,128)S(1)}, u32[]{:S(2)}, u32[]{:S(2)}) collective-permute-start(f32[4,2048]{1,0:T(4,128)S(1)} %get-tuple-element.173), channel_id=1, source_target_pairs={{24,0},{28,4},{0,8},{4,12},{8,16},{12,20},{16,24},{20,28},{25,1},{... | collective-permute-start | bytes 98312 | tf_op jit(solution)/shard_map/ppermute | solution.py:17
  58.3 131.3 %copy-start.1 = (f32[4,128,512]{2,1,0:T(8,128)S(1)}, f32[4,128,512]{2,1,0:T(8,128)}, u32[]{:S(2)}) copy-start(f32[4,128,512]{2,1,0:T(8,128)} %param.10) | copy-start | bytes 3145732
  190.5 38.8 %copy-start = (f32[4,128,512]{2,1,0:T(8,128)}, f32[4,128,512]{2,1,0:T(8,128)S(1)}, u32[]{:S(2)}) copy-start(f32[4,128,512]{2,1,0:T(8,128)S(1)} %get-tuple-element.171) | copy-start | bytes 3145732
where the time goes:
time: 231 us; the launch traced here: 229 us
  matrix products  67.3 us (29%)
  blocking collectives  49.4 us (21%)
  local copies, waits for them, and re-layouts  42.9 us (19%)
  loops' own time  25.2 us (11%)
  other arithmetic  20.4 us (9%)
  starting transfers between devices  12.7 us (5%)
  waiting for transfers between devices  10.7 us (5%)
    dot_general x40, matrix products, one_block(): jnp.dot(plane_gauss, depth_gauss, precision=lax.Precision.HIGHEST, prefer...  67.1 us
    pmax x1, blocking collectives, per_device(): highest = lax.pmax(jnp.max(new_bias), ('slab', 'walk'))  37 us
    another operation x1, loops' own time, deposit(): lax.scan(one_block, start, jnp.arange(slot_total // block_size))  25.2 us
    dynamic_slice x40, local copies, waits for them, and re-layouts, deposit(): lax.scan(one_block, start, jnp.arange(slot_total // block_size))  23.2 us
    gather x1, local copies, waits for them, and re-layouts, per_device(): picked = bias_grid.reshape(-1)[flat_place]  11.8 us
    all_to_all x1, starting transfers between devices, per_device(): lax.all_to_all(outgoing, 'slab', split_axis=1, concat_axis=1, tiled=True)  7.31 us
    psum x1, blocking collectives, per_device(): centre_value = lax.psum(jnp.where(owned, picked, 0.0), 'walk')  7.2 us
    select_n x40, other arithmetic, gaussian(): jnp.where(inside, jnp.exp(-(distance * distance) / (2.0 * spread * spread...  6.93 us
  transfers between devices with their start and end apart: 5, of which 4 were waited for; matrix products, arithmetic and copies ran while one was open for 1% of the time, Pallas kernels for 0%

commit v1 on v0

--- a/solution.py
+++ b/solution.py
@@ -1,8 +1,11 @@
+import functools
 import math
 
 import jax
 import jax.numpy as jnp
 from jax import lax
+from jax.experimental import pallas as pl
+from jax.experimental.pallas import tpu as pltpu
 from jax.sharding import PartitionSpec as P
 
 BASE_HEIGHT = 1.2
@@ -60,7 +63,7 @@
     return result.reshape(row_count, col_count, depth_count)
 
 
-def per_device(
+def by_collectives(
     bias_grid, hill_slab, hill_row, hill_col, hill_depth, hill_level, hill_count, height_levels
 ):
     rows_dev, cols_dev, depth_bins = bias_grid.shape
@@ -142,6 +145,371 @@
     return (new_bias, free_energy)
 
 
+LANES = 128
+F32 = jnp.float32
+BF16 = jnp.bfloat16
+MESH = pl.DeviceIdType.MESH
+NT = (((1,), (1,)), ((), ()))
+
+
+def wrapped(offset, extent):
+    offset = jnp.where(offset >= extent // 2, offset - extent, offset)
+    return jnp.where(offset < -(extent // 2), offset + extent, offset)
+
+
+def profile(offset, radius):
+    spread = SIGMA_SHARE * radius
+    value = jnp.exp(-(offset * offset) / (2.0 * spread * spread))
+    return jnp.where((offset >= -radius) & (offset < radius), value, 0.0)
+
+
+def halves(value):
+    high = value.astype(BF16)
+    return high, (value - high.astype(F32)).astype(BF16)
+
+
+def iota(shape, dim):
+    return lax.broadcasted_iota(jnp.int32, shape, dim).astype(F32)
+
+
+def window_kernel(
+    slabs, walks, rows, cols, levels, per_group,
+    bias_ref, slab_ref, row_ref, col_ref, depth_ref, level_ref, count_ref, table_ref,
+    new_ref, top_ref,
+    mine, hills, bias_high, bias_low, own, picked, tables, chosen,
+    left_high, left_low, right_high, right_low, near, peak, peaks,
+    a_send, a_recv, b_send, b_recv, c_send, c_recv,
+):
+    devices = slabs * walks
+    groups = devices // per_group
+    share = LANES // per_group
+    cells, depth = bias_ref.shape
+    radius = 2 * rows
+    grid_rows, grid_cols = slabs * rows, walks * cols
+    slab = lax.axis_index("slab")
+    walk = lax.axis_index("walk")
+    me = slab * walks + walk
+    first_row = (slab * rows).astype(F32)
+    first_col = (walk * cols).astype(F32)
+
+    def place(step):
+        other = lax.rem(me + step, devices)
+        return (other // walks, lax.rem(other, walks))
+
+    barrier = pltpu.get_barrier_semaphore()
+    for step in range(1, devices):
+        pl.semaphore_signal(barrier, inc=1, device_id=place(step), device_id_type=MESH)
+
+    def in_row(ref):
+        value = ref[...].astype(F32)
+        return jnp.concatenate([value[i : i + 1] for i in range(value.shape[0])], axis=1)
+
+    slots = row_ref.shape[1]
+    lane = iota((1, LANES), 1)
+    live = jnp.zeros((1, LANES), F32)
+    for i in range(row_ref.shape[0]):
+        inside = (lane >= i * slots) & (lane < i * slots + count_ref[i].astype(F32))
+        live = jnp.where(inside, 1.0, live)
+    target = in_row(slab_ref)
+    centre_row = target * rows + in_row(row_ref)
+    centre_col = in_row(col_ref)
+    centre_depth = in_row(depth_ref)
+    owner = target * walks + jnp.floor(centre_col / cols)
+    owner = jnp.where(live > 0, owner, -1.0)
+    owners = jnp.broadcast_to(owner, (LANES, LANES))
+    same = (owners == owners.T) & (iota((LANES, LANES), 0) < iota((LANES, LANES), 1))
+    rank = jnp.sum(jnp.where(same, 1.0, 0.0), axis=0, keepdims=True)
+    over = jnp.max(jnp.where((live > 0) & (rank >= share), 1.0, 0.0))
+    spot = rank + (lax.rem(me, per_group) * share).astype(F32)
+    spot = jnp.where((live > 0) & (rank < share), spot, -1.0)
+    col_high = jnp.floor(centre_col / 16.0)
+    depth_high = jnp.floor(centre_depth / 16.0)
+    fields = (
+        jnp.where(live > 0, in_row(level_ref) + 1.0, 0.0),
+        centre_row,
+        col_high,
+        centre_col - 16.0 * col_high,
+        depth_high,
+        centre_depth - 16.0 * depth_high,
+        spot,
+        live,
+    )
+    for i, field in enumerate(fields):
+        mine[i : i + 1, :] = field
+    hills[me] = mine[...]
+
+    pl.semaphore_wait(barrier, devices - 1)
+    a_copies = [
+        pltpu.make_async_remote_copy(
+            mine, hills.at[me], a_send.at[step], a_recv.at[step],
+            device_id=place(step), device_id_type=MESH,
+        )
+        for step in range(1, devices)
+    ]
+    for copy in a_copies:
+        copy.start()
+
+    high, low = halves(bias_ref[...])
+    bias_high[...] = high
+    bias_low[...] = low
+    earlier = jnp.where(
+        iota((LANES, LANES), 0) < iota((LANES, LANES), 1), 1.0, 0.0
+    ).astype(BF16)
+    one, two = (
+        lax.broadcasted_iota(jnp.int32, (devices, devices), 0),
+        lax.broadcasted_iota(jnp.int32, (devices, devices), 1),
+    )
+    before = jnp.where((one // per_group == two // per_group) & (two < one), 1.0, 0.0).astype(BF16)
+
+    for copy in a_copies:
+        copy.wait_recv()
+
+    there = hills[:, 7, :] > 0
+    hill_row = hills[:, 1, :]
+    hill_col = hills[:, 2, :] * 16.0 + hills[:, 3, :]
+    away_row = hill_row - first_row
+    away_col = hill_col - first_col
+    owned = there & (away_row >= 0) & (away_row < rows) & (away_col >= 0) & (away_col < cols)
+    own_place = jnp.where(owned, hills[:, 6, :], -1.0)
+
+    def past(away, extent, limit):
+        away = away + (radius - 1)
+        away = jnp.where(away < 0, away + extent, away)
+        away = jnp.where(away >= extent, away - extent, away)
+        return away < limit
+
+    close = (
+        there
+        & past(away_row, grid_rows, rows + 2 * radius - 1)
+        & past(away_col, grid_cols, cols + 2 * radius - 1)
+    )
+    close_one = jnp.where(close, 1.0, 0.0)
+    close_half = close_one.astype(BF16)
+    rank_in = jnp.dot(close_half, earlier, preferred_element_type=F32)
+    rank_of = jnp.sum(
+        jnp.dot(before, close_half, preferred_element_type=F32), axis=1, keepdims=True
+    )
+    close_place = jnp.where(close, rank_in + rank_of, -1.0)
+    over = jnp.maximum(over, jnp.max(jnp.where(close_place >= LANES, 1.0, 0.0)))
+
+    slot = iota((LANES, per_group * LANES), 0)
+
+    def group_fields(group):
+        parts = [hills[group * per_group + i] for i in range(per_group)]
+        return jnp.concatenate(parts, axis=1).astype(BF16)
+
+    def group_places(places, group):
+        parts = [
+            places[group * per_group + i : group * per_group + i + 1, :] for i in range(per_group)
+        ]
+        matches = slot == jnp.concatenate(parts, axis=1)
+        return jnp.where(matches, 1.0, 0.0).astype(BF16)
+
+    for group in range(groups):
+        own[group] = lax.dot_general(
+            group_fields(group), group_places(own_place, group), NT, preferred_element_type=F32
+        )
+
+    cell_id = iota((cells, LANES), 0)
+    depth_id = iota((depth, LANES), 0)
+
+    def pick(group, carry):
+        part = own[group]
+        wanted = part[4:5] * 16.0 + part[5:6]
+        select = jnp.where(depth_id == wanted, 1.0, 0.0).astype(BF16)
+        lines = jnp.dot(bias_high[...], select, preferred_element_type=F32)
+        lines = lines + jnp.dot(bias_low[...], select, preferred_element_type=F32)
+        cell = (part[1:2] - first_row) * cols + part[2:3] * 16.0 + part[3:4] - first_col
+        value = jnp.sum(jnp.where(cell_id == cell, lines, 0.0), axis=0, keepdims=True)
+        picked[pl.ds(group, 1), :] = value
+        return carry
+
+    lax.fori_loop(0, groups, pick, 0, unroll=groups <= 8)
+
+    offsets = [(i, j) for i in (-2, -1, 0, 1, 2) for j in (-1, 0, 1)]
+    b_copies = []
+    for n, (i, j) in enumerate(offsets):
+        if (i, j) == (0, 0):
+            continue
+        device = (lax.rem(slab - i + slabs, slabs), lax.rem(walk - j + walks, walks))
+        b_copies.append(
+            pltpu.make_async_remote_copy(
+                picked, tables.at[n], b_send.at[n], b_recv.at[n],
+                device_id=device, device_id_type=MESH,
+            )
+        )
+    for copy in b_copies:
+        copy.start()
+
+    depth_lane = iota((LANES, depth), 1)
+    col_id = iota((cols, LANES), 0)
+    for group in range(groups):
+        data, places = group_fields(group), group_places(close_place, group)
+        chosen[group] = lax.dot_general(data, places, NT, preferred_element_type=F32)
+        column = lax.dot_general(places, data, NT, preferred_element_type=F32)
+        at = column[:, 4:5] * 16.0 + column[:, 5:6]
+        high, low = halves(profile(wrapped(depth_lane - at, depth), radius))
+        right_high[group * LANES : (group + 1) * LANES, :] = high
+        right_low[group * LANES : (group + 1) * LANES, :] = low
+        part = chosen[group]
+        at = part[2:3] * 16.0 + part[3:4]
+        near[:, group * LANES : (group + 1) * LANES] = profile(
+            wrapped(col_id + first_col - at, grid_cols), radius
+        )
+
+    level = chosen[:, 0, :]
+    base = jnp.zeros((groups, LANES), F32)
+    for i in range(levels):
+        base = jnp.where(level == i + 1, BASE_HEIGHT * table_ref[i], base)
+    at_row = chosen[:, 1, :]
+    at_col = chosen[:, 2, :] * 16.0 + chosen[:, 3, :]
+    at_spot = chosen[:, 6, :].astype(jnp.int32)
+    slab_of = jnp.floor(at_row / rows) - slab.astype(F32)
+    walk_of = jnp.floor(at_col / cols) - walk.astype(F32)
+    slab_of = jnp.where(slab_of < -2, slab_of + slabs, slab_of)
+    slab_of = jnp.where(slab_of > 2, slab_of - slabs, slab_of)
+    walk_of = jnp.where(walk_of < -1, walk_of + walks, walk_of)
+    walk_of = jnp.where(walk_of > 1, walk_of - walks, walk_of)
+    row_parts = [
+        profile(wrapped(first_row + r - at_row, grid_rows), radius) for r in range(rows)
+    ]
+
+    for copy in b_copies:
+        copy.wait_recv()
+    centre = jnp.zeros((groups, LANES), F32)
+    for n, (i, j) in enumerate(offsets):
+        table = picked[...] if (i, j) == (0, 0) else tables[n]
+        value = jnp.take_along_axis(table, at_spot, axis=1)
+        centre = jnp.where((slab_of == i) & (walk_of == j), value, centre)
+    height = base * jnp.exp(-centre / TEMPER)
+    row_parts = [height * part for part in row_parts]
+    for r in range(rows):
+        for group in range(groups):
+            span = slice(group * LANES, (group + 1) * LANES)
+            high, low = halves(near[:, span] * row_parts[r][group : group + 1])
+            left_high[r * cols : (r + 1) * cols, span] = high
+            left_low[r * cols : (r + 1) * cols, span] = low
+
+    most = jnp.full((1, depth), -jnp.inf, F32)
+    for r in range(rows):
+        span = slice(r * cols, (r + 1) * cols)
+        added = jnp.dot(left_high[span, :], right_high[...], preferred_element_type=F32)
+        added += jnp.dot(left_low[span, :], right_high[...], preferred_element_type=F32)
+        added += jnp.dot(left_high[span, :], right_low[...], preferred_element_type=F32)
+        value = bias_ref[span, :] + added
+        new_ref[span, :] = value
+        most = jnp.maximum(most, jnp.max(value, axis=0, keepdims=True))
+    top = most[:, 0:LANES]
+    for i in range(1, depth // LANES):
+        top = jnp.maximum(top, most[:, i * LANES : (i + 1) * LANES])
+    top = jnp.where(over > 0, jnp.inf, top)
+    peak[...] = top
+    peaks[me] = top
+    c_copies = [
+        pltpu.make_async_remote_copy(
+            peak, peaks.at[me], c_send.at[step], c_recv.at[step],
+            device_id=place(step), device_id_type=MESH,
+        )
+        for step in range(1, devices)
+    ]
+    for copy in c_copies:
+        copy.start()
+    for copy in c_copies:
+        copy.wait_recv()
+    top_ref[...] = jnp.broadcast_to(jnp.max(peaks[...]), top_ref.shape)
+    for copy in a_copies + b_copies + c_copies:
+        copy.wait_send()
+
+
+def by_kernel(per_group, collective_id, slabs, walks, arrays):
+    bias_grid, hill_slab, hill_row, hill_col, hill_depth, hill_level, hill_count, table = arrays
+    rows, cols, depth = bias_grid.shape
+    devices = slabs * walks
+    groups = devices // per_group
+    total = groups * LANES
+    cells = rows * cols
+    vmem = pl.BlockSpec(memory_space=pltpu.VMEM)
+    smem = pl.BlockSpec(memory_space=pltpu.SMEM)
+    return pl.pallas_call(
+        functools.partial(
+            window_kernel, slabs, walks, rows, cols, table.shape[0], per_group
+        ),
+        out_shape=(
+            jax.ShapeDtypeStruct((cells, depth), F32),
+            jax.ShapeDtypeStruct((8, LANES), F32),
+        ),
+        in_specs=[vmem] * 6 + [smem] * 2,
+        out_specs=(vmem, vmem),
+        scratch_shapes=[
+            pltpu.VMEM((8, LANES), F32),
+            pltpu.VMEM((devices, 8, LANES), F32),
+            pltpu.VMEM((cells, depth), BF16),
+            pltpu.VMEM((cells, depth), BF16),
+            pltpu.VMEM((groups, 8, LANES), F32),
+            pltpu.VMEM((groups, LANES), F32),
+            pltpu.VMEM((15, groups, LANES), F32),
+            pltpu.VMEM((groups, 8, LANES), F32),
+            pltpu.VMEM((cells, total), BF16),
+            pltpu.VMEM((cells, total), BF16),
+            pltpu.VMEM((total, depth), BF16),
+            pltpu.VMEM((total, depth), BF16),
+            pltpu.VMEM((cols, total), F32),
+            pltpu.VMEM((1, LANES), F32),
+            pltpu.VMEM((devices, 1, LANES), F32),
+            pltpu.SemaphoreType.DMA((devices,)),
+            pltpu.SemaphoreType.DMA((devices,)),
+            pltpu.SemaphoreType.DMA((15,)),
+            pltpu.SemaphoreType.DMA((15,)),
+            pltpu.SemaphoreType.DMA((devices,)),
+            pltpu.SemaphoreType.DMA((devices,)),
+        ],
+        compiler_params=pltpu.CompilerParams(
+            collective_id=collective_id, has_side_effects=True
+        ),
+    )(
+        bias_grid.reshape(cells, depth),
+        hill_slab.reshape(hill_row.shape),
+        hill_row,
+        hill_col,
+        hill_depth,
+        hill_level,
+        hill_count,
+        table,
+    )
+
+
+def per_device(*arrays):
+    bias_grid = arrays[0]
+    shape = bias_grid.shape
+    slabs, walks = lax.axis_size("slab"), lax.axis_size("walk")
+    devices = slabs * walks
+    fits = (
+        arrays[2].size == LANES
+        and slabs >= 5
+        and walks >= 3
+        and devices <= 64
+        and devices % 4 == 0
+        and shape[1] % LANES == 0
+        and shape[1] >= 2 * shape[0]
+        and shape[2] % LANES == 0
+        and max(walks * shape[1], shape[2]) <= 4096
+        and max(slabs * shape[0], arrays[7].size) <= 255
+    )
+    if not fits:
+        return by_collectives(*arrays)
+
+    def finish(new_bias, top):
+        highest = top[0, 0]
+        return new_bias.reshape(shape), FREE_SCALE * (highest - new_bias).reshape(shape)
+
+    new_bias, top = by_kernel(4, 0, slabs, walks, arrays)
+    return lax.cond(
+        top[0, 0] == jnp.inf,
+        lambda: finish(*by_kernel(1, 1, slabs, walks, arrays)),
+        lambda: finish(new_bias, top),
+    )
+
+
 def solution(mesh):
     in_specs = (
         P("slab", "walk", None),

time: 231 us -> 36.9 us (0.16)
  matrix products: 67.3 us -> 0 us
  blocking collectives: 49.4 us -> 0 us
  local copies, waits for them, and re-layouts: 42.9 us -> 2.98 us
  Pallas kernels: 0 us -> 29.3 us
  loops' own time: 25.2 us -> 0.01 us
  other arithmetic: 20.4 us -> 3 us
  starting transfers between devices: 12.7 us -> 0 us
  waiting for transfers between devices: 10.7 us -> 0 us
    dot_general x41 -> x0, matrix products: 67.3 us -> none  [the longest x40 67.1 us: one_block(): jnp.dot(plane_gauss, depth_gauss, precision=lax.Precision.HIGHEST, prefer...]
    pmax x1 -> x0, blocking collectives: 37 us -> none  [per_device(): highest = lax.pmax(jnp.max(new_bias), ('slab', 'walk'))]
    pallas_call x0 -> x1, Pallas kernels: none -> 29.3 us  [by_kernel(): pl.pallas_call(functools.partial(window_kernel, slabs, walks, rows, cols,...]
    another operation x1, loops' own time: 25.2 us -> 0.01 us  [per_device(): lax.cond(top[0, 0] == jnp.inf, lambda: finish(*by_kernel(1, 1, slabs, wal...]
    dynamic_slice x40 -> x0, local copies, waits for them, and re-layouts: 23.2 us -> none  [deposit(): lax.scan(one_block, start, jnp.arange(slot_total // block_size))]
    gather x1 -> x0, local copies, waits for them, and re-layouts: 11.8 us -> none  [per_device(): picked = bias_grid.reshape(-1)[flat_place]]
    all_to_all x1 -> x0, starting transfers between devices: 7.31 us -> none  [per_device(): lax.all_to_all(outgoing, 'slab', split_axis=1, concat_axis=1, tiled=True)]
    psum x1 -> x0, blocking collectives: 7.2 us -> none  [per_device(): centre_value = lax.psum(jnp.where(owned, picked, 0.0), 'walk')]
  transfers between devices with their start and end apart: 5 -> 0, of which waited for: 4 -> 0; matrix products, arithmetic and copies ran while one was open for 1% -> 0% of each run, Pallas kernels for 0% -> 0%
where the time goes in v1:
time: 36.9 us; the launch traced here: 36.6 us
  Pallas kernels  29.3 us (79%)
  other arithmetic  3 us (8%)
  local copies, waits for them, and re-layouts  2.98 us (8%)
  between operations  1.41 us (4%)
    pallas_call x1, Pallas kernels, by_kernel(): pl.pallas_call(functools.partial(window_kernel, slabs, walks, rows, cols,...  29.3 us
    mul x1, other arithmetic, finish(): FREE_SCALE * (highest - new_bias).reshape(shape)  3 us
    cond x1, local copies, waits for them, and re-layouts  1.23 us

profile of v1, /device:TPU:0, one launch (start us, length us, event | category | flops | bytes accessed | tf_op | source)
XLA Modules:
  0.0 36.6 jit_solution(3335491071319996894)
XLA Ops:
  0.6 0.0 copy-start
  0.6 0.0 copy-start.3
  0.7 0.0 copy-start.4
  0.7 0.0 copy-start.5
  0.7 0.0 copy-start.6
  0.7 0.0 copy-start.8
  0.7 29.3 %shard_map.95 = (f32[512,512]{1,0:T(8,128)}, f32[8,128]{1,0:T(8,128)S(1)}) custom-call(f32[512,512]{1,0:T(8,128)} %bitcast.10, s32[2,64]{1,0:T(2,128)} %bitcast.13, s32[2,64]{1,0:T(2,128)} %row_ref.1, s32[2,64]{1,0:T(2,128)} %col_ref.1, s32[2,64]{1,0:T(2,128)} %depth_ref.1, s32[2,64]{1,0:T(2,128)} %level_ref.1, s32[2]{0:T(128)} %count_ref.1, f32[8]{0:T(128)} %table_ref.1), custom_call_target="tpu_custom_call" | custom-call | tf_op jit(solution)/shard_map/pallas_call | solution.py:433
  30.0 0.5 %slice.9 = f32[1,1]{1,0:T(1,128)} slice(f32[8,128]{1,0:T(8,128)S(1)} %get-tuple-element.35), slice={[0:1], [0:1]} | slice | bytes 8 | tf_op jit(solution)/shard_map/slice | solution.py:507
  31.1 0.0 copy-start.2
  31.1 0.0 copy-start.7
  31.1 0.0 copy-done
  31.2 0.0 copy-done.3
  31.2 0.0 copy-done.4
  31.2 0.0 copy-done.5
  31.2 0.0 copy-done.6
  31.2 0.0 copy-done.8
  31.2 0.6 %copy-done.2 = s32[2,64,1]{1,2,0:T(1,128)S(1)} copy-done((s32[2,64,1]{1,2,0:T(1,128)S(1)}, s32[2,64,1]{1,2,0:T(1,128)}, u32[]{:S(2)}) %copy-start.2) | copy-done | bytes 536
  31.8 0.0 copy-done.7
  31.8 1.2 %conditional.1 = (f32[512,512]{1,0:T(8,128)}, f32[8,128]{1,0:T(8,128)S(1)}, f32[4,128,512]{2,1,0:T(8,128)S(1)}) conditional(s32[]{:T(128)} %bitcast.2, (f32[512,512]{1,0:T(8,128)}, f32[8,128]{1,0:T(8,128)S(1)}) %shard_map.95, (f32[4,128,512]{2,1,0:T(8,128)S(1)}, s32[2,64,1]{1,2,0:T(1,128)S(1)}, s32[2,64]{1,0:T(2,128)S(1)}, ...), branch_computations={%region_0.0_spmd.clone, %region_1.0_spmd.clone} | conditional | bytes 2097176 | solution.py:506
  31.8 1.2 %copy.13 = f32[4,128,512]{2,1,0:T(8,128)S(1)} copy(f32[4,128,512]{2,1,0:T(8,128)} %bitcast.5) | data formatting | bytes 2097152 | tf_op jit(solution)/shard_map/cond
  33.0 0.0 copy-start.1
  33.0 0.6 %slice.10 = f32[1,1]{1,0:T(1,128)} slice(f32[8,128]{1,0:T(8,128)S(1)} %get-tuple-element.38), slice={[0:1], [0:1]} | slice | bytes 8 | tf_op jit(solution)/shard_map/cond/branch_0_fun/slice | solution.py:502
  33.6 3.0 %subtract_multiply_fusion = f32[512,512]{1,0:T(8,128)} fusion(f32[512,512]{1,0:T(8,128)} %get-tuple-element.37, f32[]{:T(128)} %bitcast.3), kind=kLoop, calls=%fused_computation | loop fusion | flops 524288 | bytes 2097156 | tf_op jit(solution)/shard_map/cond/branch_0_fun/mul | solution.py:503
  36.6 0.0 copy-done.1
Async XLA Ops:
  0.6 30.5 %copy-start = (f32[4,128,512]{2,1,0:T(8,128)S(1)}, f32[4,128,512]{2,1,0:T(8,128)}, u32[]{:S(2)}) copy-start(f32[4,128,512]{2,1,0:T(8,128)} %param.10) | copy-start | bytes 3145732
  0.6 30.5 %copy-start.3 = (s32[2,64]{1,0:T(2,128)S(1)}, s32[2,64]{1,0:T(2,128)}, u32[]{:S(2)}) copy-start(s32[2,64]{1,0:T(2,128)} %row_ref.1) | copy-start | bytes 1540
  0.7 30.5 %copy-start.4 = (s32[2,64]{1,0:T(2,128)S(1)}, s32[2,64]{1,0:T(2,128)}, u32[]{:S(2)}) copy-start(s32[2,64]{1,0:T(2,128)} %col_ref.1) | copy-start | bytes 1540
  0.7 30.5 %copy-start.5 = (s32[2,64]{1,0:T(2,128)S(1)}, s32[2,64]{1,0:T(2,128)}, u32[]{:S(2)}) copy-start(s32[2,64]{1,0:T(2,128)} %depth_ref.1) | copy-start | bytes 1540
  0.7 30.5 %copy-start.6 = (s32[2,64]{1,0:T(2,128)S(1)}, s32[2,64]{1,0:T(2,128)}, u32[]{:S(2)}) copy-start(s32[2,64]{1,0:T(2,128)} %level_ref.1) | copy-start | bytes 1540
  0.7 30.5 %copy-start.8 = (f32[8]{0:T(128)S(1)}, f32[8]{0:T(128)}, u32[]{:S(2)}) copy-start(f32[8]{0:T(128)} %table_ref.1) | copy-start | bytes 100
  31.1 0.7 %copy-start.2 = (s32[2,64,1]{1,2,0:T(1,128)S(1)}, s32[2,64,1]{1,2,0:T(1,128)}, u32[]{:S(2)}) copy-start(s32[2,64,1]{1,2,0:T(1,128)} %param.11) | copy-start | bytes 1540
  31.1 0.7 %copy-start.7 = (s32[2]{0:T(128)S(1)}, s32[2]{0:T(128)}, u32[]{:S(2)}) copy-start(s32[2]{0:T(128)} %count_ref.1) | copy-start | bytes 28
  33.0 3.6 %copy-start.1 = (f32[4,128,512]{2,1,0:T(8,128)}, f32[4,128,512]{2,1,0:T(8,128)S(1)}, u32[]{:S(2)}) copy-start(f32[4,128,512]{2,1,0:T(8,128)S(1)} %get-tuple-element.67) | copy-start | bytes 3145732

commit v2 on v1

--- a/solution.py
+++ b/solution.py
@@ -174,8 +174,9 @@
 
 def window_kernel(
     slabs, walks, rows, cols, levels, per_group,
-    bias_ref, slab_ref, row_ref, col_ref, depth_ref, level_ref, count_ref, table_ref,
-    new_ref, top_ref,
+    bias_in, slab_in, row_in, col_in, depth_in, level_in, count_in, table_in,
+    new_ref, top_ref, flag_ref,
+    bias_ref, slab_ref, row_ref, col_ref, depth_ref, level_ref, count_ref, table_ref, in_sems,
     mine, hills, bias_high, bias_low, own, picked, tables, chosen,
     left_high, left_low, right_high, right_low, near, peak, peaks,
     a_send, a_recv, b_send, b_recv, c_send, c_recv,
@@ -199,6 +200,19 @@
     barrier = pltpu.get_barrier_semaphore()
     for step in range(1, devices):
         pl.semaphore_signal(barrier, inc=1, device_id=place(step), device_id_type=MESH)
+
+    inputs = (
+        (slab_in, slab_ref), (row_in, row_ref), (col_in, col_ref), (depth_in, depth_ref),
+        (level_in, level_ref), (count_in, count_ref), (table_in, table_ref), (bias_in, bias_ref),
+    )
+    fetches = [
+        pltpu.make_async_copy(there, here, in_sems.at[i])
+        for i, (there, here) in enumerate(inputs)
+    ]
+    for fetch in fetches:
+        fetch.start()
+    for fetch in fetches[:-1]:
+        fetch.wait()
 
     def in_row(ref):
         value = ref[...].astype(F32)
@@ -249,6 +263,7 @@
     for copy in a_copies:
         copy.start()
 
+    fetches[-1].wait()
     high, low = halves(bias_ref[...])
     bias_high[...] = high
     bias_low[...] = low
@@ -416,7 +431,9 @@
         copy.start()
     for copy in c_copies:
         copy.wait_recv()
-    top_ref[...] = jnp.broadcast_to(jnp.max(peaks[...]), top_ref.shape)
+    highest = jnp.max(peaks[...])
+    top_ref[...] = jnp.broadcast_to(highest, top_ref.shape)
+    flag_ref[0] = jnp.where(highest == jnp.inf, 1, 0)
     for copy in a_copies + b_copies + c_copies:
         copy.wait_send()
 
@@ -428,8 +445,10 @@
     groups = devices // per_group
     total = groups * LANES
     cells = rows * cols
+    walkers = hill_row.shape
     vmem = pl.BlockSpec(memory_space=pltpu.VMEM)
     smem = pl.BlockSpec(memory_space=pltpu.SMEM)
+    hbm = pl.BlockSpec(memory_space=pltpu.HBM)
     return pl.pallas_call(
         functools.partial(
             window_kernel, slabs, walks, rows, cols, table.shape[0], per_group
@@ -437,10 +456,20 @@
         out_shape=(
             jax.ShapeDtypeStruct((cells, depth), F32),
             jax.ShapeDtypeStruct((8, LANES), F32),
+            jax.ShapeDtypeStruct((1,), jnp.int32),
         ),
-        in_specs=[vmem] * 6 + [smem] * 2,
-        out_specs=(vmem, vmem),
+        in_specs=[hbm] * 8,
+        out_specs=(vmem, vmem, smem),
         scratch_shapes=[
+            pltpu.VMEM((cells, depth), F32),
+            pltpu.VMEM(walkers, jnp.int32),
+            pltpu.VMEM(walkers, jnp.int32),
+            pltpu.VMEM(walkers, jnp.int32),
+            pltpu.VMEM(walkers, jnp.int32),
+            pltpu.VMEM(walkers, jnp.int32),
+            pltpu.SMEM(hill_count.shape, jnp.int32),
+            pltpu.SMEM(table.shape, F32),
+            pltpu.SemaphoreType.DMA((8,)),
             pltpu.VMEM((8, LANES), F32),
             pltpu.VMEM((devices, 8, LANES), F32),
             pltpu.VMEM((cells, depth), BF16),
@@ -464,7 +493,9 @@
             pltpu.SemaphoreType.DMA((devices,)),
         ],
         compiler_params=pltpu.CompilerParams(
-            collective_id=collective_id, has_side_effects=True
+            collective_id=collective_id,
+            has_side_effects=True,
+            vmem_limit_bytes=(12 + 10 * 4 // per_group) * 2**20,
         ),
     )(
         bias_grid.reshape(cells, depth),
@@ -476,6 +507,34 @@
         hill_count,
         table,
     )
+
+
+def output_kernel(new_ref, top_ref, new_out, free_out, free_ref, sems):
+    parts = 4
+    span = new_ref.shape[0] // parts
+    first = pltpu.make_async_copy(new_ref, new_out, sems.at[0])
+    first.start()
+    copies = [first]
+    for i in range(parts):
+        rows = pl.ds(i * span, span)
+        free_ref[rows, :] = FREE_SCALE * (top_ref[0:1, 0:1] - new_ref[rows, :])
+        copy = pltpu.make_async_copy(free_ref.at[rows], free_out.at[rows], sems.at[1 + i])
+        copy.start()
+        copies.append(copy)
+    for copy in copies:
+        copy.wait()
+
+
+def outputs(new_bias, top):
+    hbm = pl.BlockSpec(memory_space=pltpu.HBM)
+    return pl.pallas_call(
+        output_kernel,
+        out_shape=(jax.ShapeDtypeStruct(new_bias.shape, F32),) * 2,
+        in_specs=[pl.BlockSpec(memory_space=pltpu.VMEM)] * 2,
+        out_specs=(hbm, hbm),
+        scratch_shapes=[pltpu.VMEM(new_bias.shape, F32), pltpu.SemaphoreType.DMA((5,))],
+        compiler_params=pltpu.CompilerParams(vmem_limit_bytes=4 * 2**20),
+    )(new_bias, top)
 
 
 def per_device(*arrays):
@@ -499,13 +558,13 @@
         return by_collectives(*arrays)
 
     def finish(new_bias, top):
-        highest = top[0, 0]
-        return new_bias.reshape(shape), FREE_SCALE * (highest - new_bias).reshape(shape)
-
-    new_bias, top = by_kernel(4, 0, slabs, walks, arrays)
+        new_out, free_out = outputs(new_bias, top)
+        return new_out.reshape(shape), free_out.reshape(shape)
+
+    new_bias, top, flag = by_kernel(4, 0, slabs, walks, arrays)
     return lax.cond(
-        top[0, 0] == jnp.inf,
-        lambda: finish(*by_kernel(1, 1, slabs, walks, arrays)),
+        flag.reshape(()),
+        lambda: finish(*by_kernel(1, 1, slabs, walks, arrays)[:2]),
         lambda: finish(new_bias, top),
     )
 

time: 36.9 us -> 31.4 us (0.85)
  other arithmetic: 3 us -> 0 us
  local copies, waits for them, and re-layouts: 2.98 us -> 0.63 us
  Pallas kernels: 29.3 us -> 28.9 us
    mul x1 -> x0, other arithmetic: 3 us -> none  [finish(): FREE_SCALE * (highest - new_bias).reshape(shape)]
    pallas_call x1, Pallas kernels: 29.3 us -> 27.5 us  [by_kernel(): pl.pallas_call(functools.partial(window_kernel, slabs, walks, rows, cols,...]
    pallas_call x0 -> x1, Pallas kernels: none -> 1.35 us  [outputs(): pl.pallas_call(output_kernel, out_shape=(jax.ShapeDtypeStruct(new_bias.sh...]
    cond x1 -> x0, local copies, waits for them, and re-layouts: 1.23 us -> none
    slice x2 -> x0, local copies, waits for them, and re-layouts: 1.12 us -> none  [the longest x1 0.61 us: finish(): highest = top[0, 0]]
where the time goes in v2:
time: 31.4 us; the launch traced here: 31.2 us
  Pallas kernels  28.9 us (92%)
  between operations  1.49 us (5%)
  local copies, waits for them, and re-layouts  0.63 us (2%)
    pallas_call x1, Pallas kernels, by_kernel(): pl.pallas_call(functools.partial(window_kernel, slabs, walks, rows, cols,...  27.5 us
    pallas_call x1, Pallas kernels, outputs(): pl.pallas_call(output_kernel, out_shape=(jax.ShapeDtypeStruct(new_bias.sh...  1.35 us
    unnamed x16, local copies, waits for them, and re-layouts  0.63 us

profile of v2, /device:TPU:0, one launch (start us, length us, event | category | flops | bytes accessed | tf_op | source)
XLA Modules:
  0.0 31.2 jit_solution(9215956671093269503)
XLA Ops:
  0.6 0.0 copy-start
  0.6 0.0 copy-start.2
  0.7 0.0 copy-start.3
  0.7 0.0 copy-start.4
  0.7 0.0 copy-start.5
  0.7 0.0 copy-start.7
  0.7 27.5 %shard_map.95 = (f32[512,512]{1,0:T(8,128)S(1)}, f32[8,128]{1,0:T(8,128)S(1)}, s32[1]{0:T(128)}) custom-call(f32[512,512]{1,0:T(8,128)} %bitcast.8, s32[2,64]{1,0:T(2,128)} %bitcast.10, s32[2,64]{1,0:T(2,128)} %row_in.1, s32[2,64]{1,0:T(2,128)} %col_in.1, s32[2,64]{1,0:T(2,128)} %depth_in.1, s32[2,64]{1,0:T(2,128)} %level_in.1, s32[2]{0:T(128)} %count_in.1, ...), custom_call_target="tpu_custom_call" | custom-call | tf_op jit(solution)/shard_map/pallas_call | solution.py:452
  28.8 0.0 copy-start.1
  28.8 0.0 copy-start.6
  28.8 0.0 copy-done
  28.8 0.0 copy-done.2
  28.8 0.0 copy-done.3
  28.8 0.0 copy-done.4
  28.8 0.0 copy-done.5
  28.9 0.0 copy-done.7
  28.9 0.6 %copy-done.1 = s32[2,64,1]{1,2,0:T(1,128)S(1)} copy-done((s32[2,64,1]{1,2,0:T(1,128)S(1)}, s32[2,64,1]{1,2,0:T(1,128)}, u32[]{:S(2)}) %copy-start.1) | copy-done | bytes 536
  29.5 0.0 copy-done.6
  29.5 1.6 %conditional.1 = ((f32[512,512]{1,0:T(8,128)}, f32[512,512]{1,0:T(8,128)})) conditional(s32[]{:T(128)} %bitcast.2, (f32[512,512]{1,0:T(8,128)S(1)}, f32[8,128]{1,0:T(8,128)S(1)}) %tuple.15, (f32[4,128,512]{2,1,0:T(8,128)S(1)}, s32[2,64,1]{1,2,0:T(1,128)S(1)}, s32[2,64]{1,0:T(2,128)S(1)}, s32[2,64]{1,0:T(2,128)S(1)}, ...), branch_computations={%region_0.0_spmd.clone, %region_1.0_spmd.clone} | conditional | bytes 8 | solution.py:565
  29.5 1.3 %branch_0_fun.1 = (f32[512,512]{1,0:T(8,128)}, f32[512,512]{1,0:T(8,128)}) custom-call(f32[512,512]{1,0:T(8,128)S(1)} %get-tuple-element.48.new_ref, f32[8,128]{1,0:T(8,128)S(1)} %get-tuple-element.49.top_ref), custom_call_target="tpu_custom_call" | custom-call | tf_op jit(solution)/shard_map/cond/branch_0_fun/pallas_call | solution.py:530
Async XLA Ops:
  0.6 28.2 %copy-start = (f32[4,128,512]{2,1,0:T(8,128)S(1)}, f32[4,128,512]{2,1,0:T(8,128)}, u32[]{:S(2)}) copy-start(f32[4,128,512]{2,1,0:T(8,128)} %param.10) | copy-start | bytes 3145732
  0.6 28.2 %copy-start.2 = (s32[2,64]{1,0:T(2,128)S(1)}, s32[2,64]{1,0:T(2,128)}, u32[]{:S(2)}) copy-start(s32[2,64]{1,0:T(2,128)} %row_in.1) | copy-start | bytes 1540
  0.7 28.2 %copy-start.3 = (s32[2,64]{1,0:T(2,128)S(1)}, s32[2,64]{1,0:T(2,128)}, u32[]{:S(2)}) copy-start(s32[2,64]{1,0:T(2,128)} %col_in.1) | copy-start | bytes 1540
  0.7 28.2 %copy-start.4 = (s32[2,64]{1,0:T(2,128)S(1)}, s32[2,64]{1,0:T(2,128)}, u32[]{:S(2)}) copy-start(s32[2,64]{1,0:T(2,128)} %depth_in.1) | copy-start | bytes 1540
  0.7 28.2 %copy-start.5 = (s32[2,64]{1,0:T(2,128)S(1)}, s32[2,64]{1,0:T(2,128)}, u32[]{:S(2)}) copy-start(s32[2,64]{1,0:T(2,128)} %level_in.1) | copy-start | bytes 1540
  0.7 28.2 %copy-start.7 = (f32[8]{0:T(128)S(1)}, f32[8]{0:T(128)}, u32[]{:S(2)}) copy-start(f32[8]{0:T(128)} %table_in.1) | copy-start | bytes 100
  28.8 0.7 %copy-start.1 = (s32[2,64,1]{1,2,0:T(1,128)S(1)}, s32[2,64,1]{1,2,0:T(1,128)}, u32[]{:S(2)}) copy-start(s32[2,64,1]{1,2,0:T(1,128)} %param.11) | copy-start | bytes 1540
  28.8 0.7 %copy-start.6 = (s32[2]{0:T(128)S(1)}, s32[2]{0:T(128)}, u32[]{:S(2)}) copy-start(s32[2]{0:T(128)} %count_in.1) | copy-start | bytes 28

commit v3 on v2

--- a/solution.py
+++ b/solution.py
@@ -325,21 +325,22 @@
             group_fields(group), group_places(own_place, group), NT, preferred_element_type=F32
         )
 
-    cell_id = iota((cells, LANES), 0)
-    depth_id = iota((depth, LANES), 0)
-
-    def pick(group, carry):
-        part = own[group]
+    cell_id = iota((cells, 2 * LANES), 0)
+    depth_id = iota((depth, 2 * LANES), 0)
+
+    def pick(pair, carry):
+        part = jnp.concatenate([own[2 * pair], own[2 * pair + 1]], axis=1)
         wanted = part[4:5] * 16.0 + part[5:6]
         select = jnp.where(depth_id == wanted, 1.0, 0.0).astype(BF16)
         lines = jnp.dot(bias_high[...], select, preferred_element_type=F32)
         lines = lines + jnp.dot(bias_low[...], select, preferred_element_type=F32)
         cell = (part[1:2] - first_row) * cols + part[2:3] * 16.0 + part[3:4] - first_col
         value = jnp.sum(jnp.where(cell_id == cell, lines, 0.0), axis=0, keepdims=True)
-        picked[pl.ds(group, 1), :] = value
+        picked[pl.ds(2 * pair, 1), :] = value[:, :LANES]
+        picked[pl.ds(2 * pair + 1, 1), :] = value[:, LANES:]
         return carry
 
-    lax.fori_loop(0, groups, pick, 0, unroll=groups <= 8)
+    lax.fori_loop(0, groups // 2, pick, 0, unroll=groups <= 8)
 
     offsets = [(i, j) for i in (-2, -1, 0, 1, 2) for j in (-1, 0, 1)]
     b_copies = []
@@ -405,15 +406,12 @@
             left_high[r * cols : (r + 1) * cols, span] = high
             left_low[r * cols : (r + 1) * cols, span] = low
 
-    most = jnp.full((1, depth), -jnp.inf, F32)
-    for r in range(rows):
-        span = slice(r * cols, (r + 1) * cols)
-        added = jnp.dot(left_high[span, :], right_high[...], preferred_element_type=F32)
-        added += jnp.dot(left_low[span, :], right_high[...], preferred_element_type=F32)
-        added += jnp.dot(left_high[span, :], right_low[...], preferred_element_type=F32)
-        value = bias_ref[span, :] + added
-        new_ref[span, :] = value
-        most = jnp.maximum(most, jnp.max(value, axis=0, keepdims=True))
+    added = jnp.dot(left_high[...], right_high[...], preferred_element_type=F32)
+    added += jnp.dot(left_low[...], right_high[...], preferred_element_type=F32)
+    added += jnp.dot(left_high[...], right_low[...], preferred_element_type=F32)
+    value = bias_ref[...] + added
+    new_ref[...] = value
+    most = jnp.max(value, axis=0, keepdims=True)
     top = most[:, 0:LANES]
     for i in range(1, depth // LANES):
         top = jnp.maximum(top, most[:, i * LANES : (i + 1) * LANES])
@@ -547,7 +545,7 @@
         and slabs >= 5
         and walks >= 3
         and devices <= 64
-        and devices % 4 == 0
+        and devices % 8 == 0
         and shape[1] % LANES == 0
         and shape[1] >= 2 * shape[0]
         and shape[2] % LANES == 0

time: 31.4 us -> 30.2 us (0.962)
  Pallas kernels: 28.9 us -> 27.6 us
    pallas_call x1, Pallas kernels: 27.5 us -> 26.3 us  [by_kernel(): pl.pallas_call(functools.partial(window_kernel, slabs, walks, rows, cols,...]
where the time goes in v3:
time: 30.2 us; the launch traced here: 30 us
  Pallas kernels  27.6 us (91%)
  between operations  1.49 us (5%)
  local copies, waits for them, and re-layouts  0.63 us (2%)
    pallas_call x1, Pallas kernels, by_kernel(): pl.pallas_call(functools.partial(window_kernel, slabs, walks, rows, cols,...  26.3 us
    pallas_call x1, Pallas kernels, outputs(): pl.pallas_call(output_kernel, out_shape=(jax.ShapeDtypeStruct(new_bias.sh...  1.35 us
    unnamed x16, local copies, waits for them, and re-layouts  0.63 us

profile of v3, /device:TPU:0, one launch (start us, length us, event | category | flops | bytes accessed | tf_op | source)
XLA Modules:
  0.0 30.0 jit_solution(331712081139816158)
XLA Ops:
  0.6 0.0 copy-start
  0.6 0.0 copy-start.2
  0.7 0.0 copy-start.3
  0.7 0.0 copy-start.4
  0.7 0.0 copy-start.5
  0.7 0.0 copy-start.7
  0.7 26.3 %shard_map.95 = (f32[512,512]{1,0:T(8,128)S(1)}, f32[8,128]{1,0:T(8,128)S(1)}, s32[1]{0:T(128)}) custom-call(f32[512,512]{1,0:T(8,128)} %bitcast.8, s32[2,64]{1,0:T(2,128)} %bitcast.10, s32[2,64]{1,0:T(2,128)} %row_in.1, s32[2,64]{1,0:T(2,128)} %col_in.1, s32[2,64]{1,0:T(2,128)} %depth_in.1, s32[2,64]{1,0:T(2,128)} %level_in.1, s32[2]{0:T(128)} %count_in.1, ...), custom_call_target="tpu_custom_call" | custom-call | tf_op jit(solution)/shard_map/pallas_call | solution.py:450
  27.6 0.0 copy-start.1
  27.6 0.0 copy-start.6
  27.6 0.0 copy-done
  27.6 0.0 copy-done.2
  27.6 0.0 copy-done.3
  27.6 0.0 copy-done.4
  27.6 0.0 copy-done.5
  27.6 0.0 copy-done.7
  27.6 0.6 %copy-done.1 = s32[2,64,1]{1,2,0:T(1,128)S(1)} copy-done((s32[2,64,1]{1,2,0:T(1,128)S(1)}, s32[2,64,1]{1,2,0:T(1,128)}, u32[]{:S(2)}) %copy-start.1) | copy-done | bytes 536
  28.2 0.0 copy-done.6
  28.2 1.6 %conditional.1 = ((f32[512,512]{1,0:T(8,128)}, f32[512,512]{1,0:T(8,128)})) conditional(s32[]{:T(128)} %bitcast.2, (f32[512,512]{1,0:T(8,128)S(1)}, f32[8,128]{1,0:T(8,128)S(1)}) %tuple.15, (f32[4,128,512]{2,1,0:T(8,128)S(1)}, s32[2,64,1]{1,2,0:T(1,128)S(1)}, s32[2,64]{1,0:T(2,128)S(1)}, s32[2,64]{1,0:T(2,128)S(1)}, ...), branch_computations={%region_0.0_spmd.clone, %region_1.0_spmd.clone} | conditional | bytes 8 | solution.py:563
  28.2 1.3 %branch_0_fun.1 = (f32[512,512]{1,0:T(8,128)}, f32[512,512]{1,0:T(8,128)}) custom-call(f32[512,512]{1,0:T(8,128)S(1)} %get-tuple-element.48.new_ref, f32[8,128]{1,0:T(8,128)S(1)} %get-tuple-element.49.top_ref), custom_call_target="tpu_custom_call" | custom-call | tf_op jit(solution)/shard_map/cond/branch_0_fun/pallas_call | solution.py:528
Async XLA Ops:
  0.6 27.0 %copy-start = (f32[4,128,512]{2,1,0:T(8,128)S(1)}, f32[4,128,512]{2,1,0:T(8,128)}, u32[]{:S(2)}) copy-start(f32[4,128,512]{2,1,0:T(8,128)} %param.10) | copy-start | bytes 3145732
  0.6 27.0 %copy-start.2 = (s32[2,64]{1,0:T(2,128)S(1)}, s32[2,64]{1,0:T(2,128)}, u32[]{:S(2)}) copy-start(s32[2,64]{1,0:T(2,128)} %row_in.1) | copy-start | bytes 1540
  0.7 27.0 %copy-start.3 = (s32[2,64]{1,0:T(2,128)S(1)}, s32[2,64]{1,0:T(2,128)}, u32[]{:S(2)}) copy-start(s32[2,64]{1,0:T(2,128)} %col_in.1) | copy-start | bytes 1540
  0.7 27.0 %copy-start.4 = (s32[2,64]{1,0:T(2,128)S(1)}, s32[2,64]{1,0:T(2,128)}, u32[]{:S(2)}) copy-start(s32[2,64]{1,0:T(2,128)} %depth_in.1) | copy-start | bytes 1540
  0.7 27.0 %copy-start.5 = (s32[2,64]{1,0:T(2,128)S(1)}, s32[2,64]{1,0:T(2,128)}, u32[]{:S(2)}) copy-start(s32[2,64]{1,0:T(2,128)} %level_in.1) | copy-start | bytes 1540
  0.7 27.0 %copy-start.7 = (f32[8]{0:T(128)S(1)}, f32[8]{0:T(128)}, u32[]{:S(2)}) copy-start(f32[8]{0:T(128)} %table_in.1) | copy-start | bytes 100
  27.6 0.7 %copy-start.1 = (s32[2,64,1]{1,2,0:T(1,128)S(1)}, s32[2,64,1]{1,2,0:T(1,128)}, u32[]{:S(2)}) copy-start(s32[2,64,1]{1,2,0:T(1,128)} %param.11) | copy-start | bytes 1540
  27.6 0.7 %copy-start.6 = (s32[2]{0:T(128)S(1)}, s32[2]{0:T(128)}, u32[]{:S(2)}) copy-start(s32[2]{0:T(128)} %count_in.1) | copy-start | bytes 28

commit v4 on v3

--- a/solution.py
+++ b/solution.py
@@ -197,8 +197,9 @@
         other = lax.rem(me + step, devices)
         return (other // walks, lax.rem(other, walks))
 
+    steps = sorted(range(1, devices), key=lambda step: -min(step, devices - step))
     barrier = pltpu.get_barrier_semaphore()
-    for step in range(1, devices):
+    for step in steps:
         pl.semaphore_signal(barrier, inc=1, device_id=place(step), device_id_type=MESH)
 
     inputs = (
@@ -258,7 +259,7 @@
             mine, hills.at[me], a_send.at[step], a_recv.at[step],
             device_id=place(step), device_id_type=MESH,
         )
-        for step in range(1, devices)
+        for step in steps
     ]
     for copy in a_copies:
         copy.start()
@@ -344,7 +345,7 @@
 
     offsets = [(i, j) for i in (-2, -1, 0, 1, 2) for j in (-1, 0, 1)]
     b_copies = []
-    for n, (i, j) in enumerate(offsets):
+    for n, (i, j) in sorted(enumerate(offsets), key=lambda item: -abs(item[1][0])):
         if (i, j) == (0, 0):
             continue
         device = (lax.rem(slab - i + slabs, slabs), lax.rem(walk - j + walks, walks))
@@ -423,7 +424,7 @@
             peak, peaks.at[me], c_send.at[step], c_recv.at[step],
             device_id=place(step), device_id_type=MESH,
         )
-        for step in range(1, devices)
+        for step in steps
     ]
     for copy in c_copies:
         copy.start()

time: 30.2 us -> 30.1 us (level)
  no operation moved by 1% of the time
where the time goes in v4:
time: 30.1 us; the launch traced here: 30 us
  Pallas kernels  27.6 us (92%)
  between operations  1.49 us (5%)
  local copies, waits for them, and re-layouts  0.63 us (2%)
    pallas_call x1, Pallas kernels, by_kernel(): pl.pallas_call(functools.partial(window_kernel, slabs, walks, rows, cols,...  26.3 us
    pallas_call x1, Pallas kernels, outputs(): pl.pallas_call(output_kernel, out_shape=(jax.ShapeDtypeStruct(new_bias.sh...  1.35 us
    unnamed x16, local copies, waits for them, and re-layouts  0.63 us

profile of v4, /device:TPU:0, one launch (start us, length us, event | category | flops | bytes accessed | tf_op | source)
XLA Modules:
  0.0 30.0 jit_solution(17924087280762539887)
XLA Ops:
  0.6 0.0 copy-start
  0.6 0.0 copy-start.2
  0.7 0.0 copy-start.3
  0.7 0.0 copy-start.4
  0.7 0.0 copy-start.5
  0.7 0.0 copy-start.7
  0.7 26.3 %shard_map.95 = (f32[512,512]{1,0:T(8,128)S(1)}, f32[8,128]{1,0:T(8,128)S(1)}, s32[1]{0:T(128)}) custom-call(f32[512,512]{1,0:T(8,128)} %bitcast.8, s32[2,64]{1,0:T(2,128)} %bitcast.10, s32[2,64]{1,0:T(2,128)} %row_in.1, s32[2,64]{1,0:T(2,128)} %col_in.1, s32[2,64]{1,0:T(2,128)} %depth_in.1, s32[2,64]{1,0:T(2,128)} %level_in.1, s32[2]{0:T(128)} %count_in.1, ...), custom_call_target="tpu_custom_call" | custom-call | tf_op jit(solution)/shard_map/pallas_call | solution.py:451
  27.5 0.0 copy-start.1
  27.5 0.0 copy-start.6
  27.6 0.0 copy-done
  27.6 0.0 copy-done.2
  27.6 0.0 copy-done.3
  27.6 0.0 copy-done.4
  27.6 0.0 copy-done.5
  27.6 0.0 copy-done.7
  27.6 0.6 %copy-done.1 = s32[2,64,1]{1,2,0:T(1,128)S(1)} copy-done((s32[2,64,1]{1,2,0:T(1,128)S(1)}, s32[2,64,1]{1,2,0:T(1,128)}, u32[]{:S(2)}) %copy-start.1) | copy-done | bytes 536
  28.2 0.0 copy-done.6
  28.2 1.6 %conditional.1 = ((f32[512,512]{1,0:T(8,128)}, f32[512,512]{1,0:T(8,128)})) conditional(s32[]{:T(128)} %bitcast.2, (f32[512,512]{1,0:T(8,128)S(1)}, f32[8,128]{1,0:T(8,128)S(1)}) %tuple.15, (f32[4,128,512]{2,1,0:T(8,128)S(1)}, s32[2,64,1]{1,2,0:T(1,128)S(1)}, s32[2,64]{1,0:T(2,128)S(1)}, s32[2,64]{1,0:T(2,128)S(1)}, ...), branch_computations={%region_0.0_spmd.clone, %region_1.0_spmd.clone} | conditional | bytes 8 | solution.py:564
  28.2 1.3 %branch_0_fun.1 = (f32[512,512]{1,0:T(8,128)}, f32[512,512]{1,0:T(8,128)}) custom-call(f32[512,512]{1,0:T(8,128)S(1)} %get-tuple-element.48.new_ref, f32[8,128]{1,0:T(8,128)S(1)} %get-tuple-element.49.top_ref), custom_call_target="tpu_custom_call" | custom-call | tf_op jit(solution)/shard_map/cond/branch_0_fun/pallas_call | solution.py:529
Async XLA Ops:
  0.6 26.9 %copy-start = (f32[4,128,512]{2,1,0:T(8,128)S(1)}, f32[4,128,512]{2,1,0:T(8,128)}, u32[]{:S(2)}) copy-start(f32[4,128,512]{2,1,0:T(8,128)} %param.10) | copy-start | bytes 3145732
  0.6 26.9 %copy-start.2 = (s32[2,64]{1,0:T(2,128)S(1)}, s32[2,64]{1,0:T(2,128)}, u32[]{:S(2)}) copy-start(s32[2,64]{1,0:T(2,128)} %row_in.1) | copy-start | bytes 1540
  0.7 26.9 %copy-start.3 = (s32[2,64]{1,0:T(2,128)S(1)}, s32[2,64]{1,0:T(2,128)}, u32[]{:S(2)}) copy-start(s32[2,64]{1,0:T(2,128)} %col_in.1) | copy-start | bytes 1540
  0.7 26.9 %copy-start.4 = (s32[2,64]{1,0:T(2,128)S(1)}, s32[2,64]{1,0:T(2,128)}, u32[]{:S(2)}) copy-start(s32[2,64]{1,0:T(2,128)} %depth_in.1) | copy-start | bytes 1540
  0.7 26.9 %copy-start.5 = (s32[2,64]{1,0:T(2,128)S(1)}, s32[2,64]{1,0:T(2,128)}, u32[]{:S(2)}) copy-start(s32[2,64]{1,0:T(2,128)} %level_in.1) | copy-start | bytes 1540
  0.7 26.9 %copy-start.7 = (f32[8]{0:T(128)S(1)}, f32[8]{0:T(128)}, u32[]{:S(2)}) copy-start(f32[8]{0:T(128)} %table_in.1) | copy-start | bytes 100
  27.5 0.7 %copy-start.1 = (s32[2,64,1]{1,2,0:T(1,128)S(1)}, s32[2,64,1]{1,2,0:T(1,128)}, u32[]{:S(2)}) copy-start(s32[2,64,1]{1,2,0:T(1,128)} %param.11) | copy-start | bytes 1540
  27.5 0.7 %copy-start.6 = (s32[2]{0:T(128)S(1)}, s32[2]{0:T(128)}, u32[]{:S(2)}) copy-start(s32[2]{0:T(128)} %count_in.1) | copy-start | bytes 28
